TPU v7x, 32 devices: a whole 2x2x4 slice. The times are simulated.
32 devices in a mesh: rep: 8 (over y, x, core), shard: 4 (over z).
Axes of the slice: x: 2, y: 2, z: 4, core: 2. Of those that a mesh axis runs over, the one named last changes fastest.
Arguments:
- features: bfloat16 [32, 28, 28, 704], P(('rep', 'shard')), may hold values from -6 to 6
- cotangent: bfloat16 [32, 28, 28, 704], P(('rep', 'shard')), may hold values from -6 to 6
- dw_kernel: float32 [49, 704], replicated, may hold values from -0.875 to 0.875
- norm_gain: float32 [704], replicated, may hold values from 0.1 to 1.9
- w_expand: bfloat16 [2816, 704], P('shard'), may hold values from -1 to 1
- grn_gamma: float32 [2816], replicated, may hold values from -3 to 3
- grn_beta: float32 [2816], replicated, may hold values from -3 to 3
- w_reduce: bfloat16 [2816, 704], P('shard'), may hold values from -0.109375 to 0.109375
Outputs:
- block_out: bfloat16 [32, 28, 28, 704], P(('rep', 'shard'))
- grad_features: bfloat16 [32, 28, 28, 704], P(('rep', 'shard'))
- grad_kernel: float32 [49, 704], replicated
- grad_gain: float32 [704], replicated
- grad_expand: float32 [2816, 704], P('shard')
- grad_gamma: float32 [2816], replicated
- grad_beta: float32 [2816], replicated
- grad_reduce: float32 [2816, 704], P('shard')
All inputs are finite; a program needn't handle non-finite values.
Results may differ from a plain program's by a relative error of at most 0.02.
Values may be sent and summed in bfloat16 or wider, within the bound.
A program may use at most 320 MiB of HBM per device.

v0:
```python
import jax
import jax.numpy as jnp
from jax import lax
from jax.sharding import PartitionSpec as P


def stem_norm(images, dw_kernel, norm_gain):
    height = images.shape[1]
    breadth = images.shape[2]
    padded = jnp.pad(images, ((0, 0), (3, 3), (3, 3), (0, 0)))
    filtered = jnp.zeros_like(images)
    for offset_row in range(7):
        for offset_col in range(7):
            filtered = (
                filtered
                + dw_kernel[offset_row * 7 + offset_col]
                * padded[:, offset_row : offset_row + height, offset_col : offset_col + breadth, :]
            )
    centre = jnp.mean(filtered, axis=-1, keepdims=True)
    shifted = filtered - centre
    spread = jnp.mean(shifted * shifted, axis=-1, keepdims=True)
    return shifted * lax.rsqrt(spread + 1e-06) * norm_gain


def hidden_map(preact, grn_gamma, grn_beta):
    active = jax.nn.gelu(preact, approximate=False)
    energy = jnp.sqrt(jnp.sum(active * active, axis=(1, 2), keepdims=True) + 1e-06)
    ratio_map = energy / (jnp.mean(energy, axis=-1, keepdims=True) + 1e-06)
    return grn_gamma * (active * ratio_map) + grn_beta + active


def contract_rows(left_cols, right_cols):
    return lax.dot_general(
        left_cols, right_cols, (((0,), (0,)), ((), ())), preferred_element_type=jnp.float32
    )


def against_rows(left_cols, pieces):
    return lax.dot_general(
        left_cols, pieces, (((1,), (1,)), ((), ())), preferred_element_type=jnp.float32
    )


def shards(features, cotangent, dw_kernel, norm_gain, w_expand, grn_gamma, grn_beta, w_reduce):
    rep_count = lax.axis_size("rep")
    shard_count = lax.axis_size("shard")
    channels = w_expand.shape[1]
    images = features.astype(jnp.float32)
    normed, stem_back = jax.vjp(stem_norm, images, dw_kernel, norm_gain)
    normed_b = normed.astype(jnp.bfloat16)
    tokens = images.shape[0] * images.shape[1] * images.shape[2]
    rows_in = normed_b.reshape(tokens, channels)
    upstream = cotangent.reshape(tokens, channels)
    preact = against_rows(rows_in, lax.all_gather(w_expand, "shard", axis=0, tiled=True))
    hidden_shape = images.shape[:3] + (preact.shape[1],)
    mapped, map_back = jax.vjp(hidden_map, preact.reshape(hidden_shape), grn_gamma, grn_beta)
    mapped_b = mapped.astype(jnp.bfloat16).reshape(tokens, preact.shape[1])
    selected = mapped_b
    branch = jnp.dot(
        selected,
        lax.all_gather(w_reduce, "shard", axis=0, tiled=True),
        preferred_element_type=jnp.float32,
    )
    back_mapped = against_rows(upstream, lax.all_gather(w_reduce, "shard", axis=0, tiled=True))
    block_out = (images + branch.reshape(images.shape)).astype(jnp.bfloat16)
    back_preact, back_gamma, back_beta = map_back(back_mapped.reshape(hidden_shape))
    back_preact_b = back_preact.astype(jnp.bfloat16).reshape(tokens, preact.shape[1])
    selected = back_preact_b
    back_normed = jnp.dot(
        selected,
        lax.all_gather(w_expand, "shard", axis=0, tiled=True),
        preferred_element_type=jnp.float32,
    )
    back_images, back_kernel, back_gain = stem_back(back_normed.reshape(images.shape))
    grad_features = (cotangent.astype(jnp.float32) + back_images).astype(jnp.bfloat16)
    partial_sum = lax.psum_scatter(
        jnp.concatenate(
            [contract_rows(back_preact_b, rows_in), contract_rows(mapped_b, upstream)], axis=1
        ).astype(jnp.bfloat16),
        "shard",
        scatter_dimension=0,
        tiled=True,
    )
    summed = lax.psum(partial_sum, "rep").astype(jnp.float32)
    reduced = lax.psum((back_kernel, back_gain, back_gamma, back_beta), ("rep", "shard"))
    inverse = 1.0 / (features.shape[0] * rep_count * shard_count)
    grad_expand = summed[:, :channels] * inverse
    grad_reduce = summed[:, channels:] * inverse
    return (
        block_out,
        grad_features,
        reduced[0] * inverse,
        reduced[1] * inverse,
        grad_expand,
        reduced[2] * inverse,
        reduced[3] * inverse,
        grad_reduce,
    )


def solution(mesh):
    return jax.shard_map(
        shards,
        mesh=mesh,
        in_specs=(
            P(("rep", "shard"), None, None, None),
            P(("rep", "shard"), None, None, None),
            P(),
            P(),
            P("shard", None),
            P(),
            P(),
            P("shard", None),
        ),
        out_specs=(
            P(("rep", "shard"), None, None, None),
            P(("rep", "shard"), None, None, None),
            P(),
            P(),
            P("shard", None),
            P(),
            P(),
            P("shard", None),
        ),
        check_vma=False,
    )
```

profile of v0, /device:TPU:0, one launch (start us, length us, event | category | flops | bytes accessed | tf_op | source)
XLA Modules:
  0.0 607.8 jit_solution(16714481349532513153)
XLA Ops:
  7.2 0.7 all-gather.3.cloned.1.call-update
  8.0 0.7 all-gather.5.cloned.1.call-update
  8.7 1.1 slice_reduce_fusion.46
  9.9 1.5 slice_reduce_fusion.48
  11.5 1.4 slice_reduce_fusion.47
  13.1 1.4 reshape.864
  14.5 1.9 convert_element_type.43
  16.7 69.4 %fusion.20 = (f32[28,28]{1,0:T(8,128)S(1)}, f32[1,28,28,704]{3,2,1,0:T(8,128)S(1)}) fusion(f32[704]{0:T(1024)S(1)} %get-tuple-element.133, f32[704]{0:T(1024)S(1)} %get-tuple-element.134, f32[704]{0:T(1024)S(1)} %get-tuple-element.87, f32[704]{0:T(1024)S(1)} %get-tuple-element.88, f32[704]{0:T(1024)S(1)} %get-tuple-element.89, ...), kind=kLoop, calls=%fused_computation.260 | loop fusion | flops 54088944 | bytes 4556608 | tf_op jit(solution)/shard_map/jvp()/reduce_sum | solution.py:19
  86.9 1.5 multiply_convert_fusion
  88.3 3.2 reshape.862
  91.6 3.7 all-gather.3.cloned.1.call-done
  95.2 26.2 %multiply_reduce_fusion.2 = (f32[2816]{0:T(1024)S(1)}, f32[784,2816]{1,0:T(8,128)}, f32[784,2816]{1,0:T(8,128)}) fusion(bf16[784,704]{1,0:T(8,128)(2,1)} %reshape.862, bf16[2816,704]{1,0:T(8,128)(2,1)} %all-gather.3.cloned.1.call-done), kind=kOutput, calls=%fused_computation.55 | convolution fusion | flops 3254211840 | bytes 22742016 | tf_op jit(solution)/shard_map/dot_general | solution.py:39
  121.4 0.6 fusion.18
  122.7 55.5 %all-gather.5.cloned.1.call-done = bf16[2816,704]{1,0:T(8,128)(2,1)} async-done(((bf16[704,704]{1,0:T(8,128)(2,1)}), bf16[2816,704]{1,0:T(8,128)(2,1)}) %all-gather.5.cloned.1.call-update) | async-done | bytes 3964944 | tf_op jit(solution)/shard_map/all_gather | solution.py:61
  178.2 12.9 %multiply_reduce_fusion = (f32[2816]{0:T(1024)S(1)}, f32[2816]{0:T(1024)S(1)}, f32[2816]{0:T(1024)S(1)}, f32[784,2816]{1,0:T(8,128)}) fusion(f32[2816]{0:T(1024)S(1)} %fusion.17, f32[784,2816]{1,0:T(8,128)} %get-tuple-element.140, f32[784,2816]{1,0:T(8,128)} %get-tuple-element.196, f32[2816]{0:T(1024)S(1)} %copy-done.82, bf16[784,704]{1,0:T(8,128)(2,1)} %reshape.864, ...), kind=kOutput, calls=%fused_computation.51 | convolution fusion | flops 3128364800 | bytes 31618048 | tf_op jit(solution)/shard_map/dot_general | solution.py:39
  191.1 0.6 multiply_reduce_fusion.55
  192.4 15.7 %add_convert_fusion = (bf16[784,2816]{1,0:T(8,128)(2,1)}, bf16[784,2816]{1,0:T(8,128)(2,1)}) fusion(f32[784,2816]{1,0:T(8,128)} %get-tuple-element.140, f32[784,2816]{1,0:T(8,128)} %get-tuple-element.197, f32[784,2816]{1,0:T(8,128)} %get-tuple-element.196, f32[2816]{0:T(1024)S(1)} %multiply_multiply_fusion.7, f32[2816]{0:T(1024)S(1)} %fusion.17, ...), kind=kLoop, calls=%fused_computation.52 | loop fusion | flops 57401344 | bytes 35368960 | tf_op jit(solution)/shard_map/convert_element_type | solution.py:67
  208.1 7.1 %reshape.863 = bf16[28,28,2816]{2,1,0:T(8,128)(2,1)} reshape(bf16[784,2816]{1,0:T(8,128)(2,1)} %get-tuple-element.144) | data formatting | bytes 8830976 | tf_op jit(solution)/shard_map/reshape.574
  215.1 9.1 %bitcast_convert_fusion = bf16[2816,704]{0,1:T(8,128)(2,1)} fusion(bf16[28,28,2816]{2,1,0:T(8,128)(2,1)} %reshape.863, bf16[1,28,28,704]{3,2,1,0:T(8,128)(2,1)} %param.9), kind=kOutput, calls=%fused_computation.71 | convolution fusion | flops 3110486016 | bytes 9484288 | tf_op jit(solution)/shard_map/dot_general | solution.py:33
  224.3 6.8 %convert_element_type.50 = bf16[28,28,2816]{2,1,0:T(8,128)(2,1)} reshape(bf16[784,2816]{1,0:T(8,128)(2,1)} %get-tuple-element.143) | data formatting | bytes 8830976 | tf_op jit(solution)/shard_map/convert_element_type | solution.py:67
  231.1 9.0 %bitcast_convert_fusion.1 = bf16[2816,704]{0,1:T(8,128)(2,1)} fusion(bf16[28,28,2816]{2,1,0:T(8,128)(2,1)} %convert_element_type.50, bf16[1,28,28,704]{3,2,1,0:T(8,128)(2,1)} %multiply_convert_fusion), kind=kOutput, calls=%fused_computation.72 | convolution fusion | flops 3110486016 | bytes 9484288 | tf_op jit(solution)/shard_map/dot_general | solution.py:33
  240.1 7.1 %pad_maximum_fusion = bf16[2816,1408]{0,1:T(8,128)(2,1)} fusion(bf16[2816,704]{0,1:T(8,128)(2,1)} %bitcast_convert_fusion, bf16[2816,704]{0,1:T(8,128)(2,1)} %bitcast_convert_fusion.1), kind=kLoop, calls=%fused_computation.70 | loop fusion | flops 15859712 | bytes 15859712 | tf_op jit(solution)/shard_map/concatenate | solution.py:77
  247.2 11.4 %copy.22 = bf16[2816,1408]{1,0:T(8,128)(2,1)} copy(bf16[2816,1408]{0,1:T(8,128)(2,1)} %pad_maximum_fusion) | data formatting | bytes 15859712
  258.7 8.6 %fusion.21 = f32[784,704]{1,0:T(8,128)} fusion(bf16[784,2816]{1,0:T(8,128)(2,1)} %get-tuple-element.143, bf16[2816,704]{1,0:T(8,128)(2,1)} %all-gather.3.cloned.1.call-done), kind=kOutput, calls=%fused_computation.261 | convolution fusion | flops 3108503552 | bytes 10588160 | tf_op jit(solution)/shard_map/dot_general | solution.py:69
  267.2 3.8 reshape.865
  271.0 2.6 multiply_reduce_fusion.53
  273.7 1.4 multiply_reduce_fusion.3
  275.9 8.0 %multiply_reduce_fusion.50 = (f32[704]{0:T(1024)S(1)}, f32[704]{0:T(1024)S(1)}, f32[704]{0:T(1024)S(1)}, f32[704]{0:T(1024)S(1)}, f32[704]{0:T(1024)S(1)}, /*ind...) fusion(f32[1,28,28,704]{3,2,1,0:T(8,128)S(1)} %copy-done.2, ...), kind=kLoop, calls=%fused_computation.134 | loop fusion | flops 18756672 | bytes 9986816 | tf_op jit(solution)/shard_map/transpose(jvp())/reduce_sum | solution.py:16
  284.0 11.9 %multiply_reduce_fusion.52 = (f32[704]{0:T(1024)S(1)}, f32[704]{0:T(1024)S(1)}, f32[704]{0:T(1024)S(1)}, f32[704]{0:T(1024)S(1)}, f32[704]{0:T(1024)S(1)}, /*ind...) fusion(f32[1,28,28,704]{3,2,1,0:T(8,128)S(1)} %get-tuple-elemen, ...), kind=kLoop, calls=%fused_computation.136 | loop fusion | flops 19857024 | bytes 4466176 | tf_op jit(solution)/shard_map/transpose(jvp())/reduce_sum | solution.py:16
  296.0 11.3 %multiply_reduce_fusion.51 = (f32[704]{0:T(1024)S(1)}, f32[704]{0:T(1024)S(1)}, f32[704]{0:T(1024)S(1)}, f32[704]{0:T(1024)S(1)}, f32[704]{0:T(1024)S(1)}, /*ind...) fusion(f32[1,28,28,704]{3,2,1,0:T(8,128)S(1)} %get-tuple-elemen, ...), kind=kLoop, calls=%fused_computation.135 | loop fusion | flops 19857024 | bytes 4466176 | tf_op jit(solution)/shard_map/transpose(jvp())/reduce_sum | solution.py:16
  307.7 1.0 pad_add_fusion.7
  308.9 13.6 %broadcast_multiply_fusion.2 = (f32[1,28,28,704]{3,2,1,0:T(8,128)}, f32[1,28,28,704]{3,2,1,0:T(8,128)}, f32[1,28,28,704]{3,2,1,0:T(8,128)}, f32[1,28,28,704]{3,2...) fusion(f32[1,28,28,704]{3,2,1,0:T(8,128)} %copy-done, ...), kind=kLoop, calls=%fused_computation.148 | loop fusion | flops 7175168 | bytes 30945024 | tf_op jit(solution)/shard_map/transpose(jvp())/mul | solution.py:16
  322.9 16.1 %broadcast_multiply_fusion.1 = (f32[1,28,28,704]{3,2,1,0:T(8,128)}, f32[1,28,28,704]{3,2,1,0:T(8,128)}, f32[1,28,28,704]{3,2,1,0:T(8,128)}, f32[1,28,28,704]{3,2...) fusion(f32[1,28,28,704]{3,2,1,0:T(8,128)S(1)} %copy-done.1, ...), kind=kLoop, calls=%fused_computation.147 | loop fusion | flops 9934848 | bytes 41997824 | tf_op jit(solution)/shard_map/transpose(jvp())/mul | solution.py:16
  339.1 16.3 %broadcast_multiply_fusion = (f32[1,28,28,704]{3,2,1,0:T(8,128)}, f32[1,28,28,704]{3,2,1,0:T(8,128)}, f32[1,28,28,704]{3,2,1,0:T(8,128)}, f32[1,28,28,704]{3,2,1...) fusion(f32[1,28,28,704]{3,2,1,0:T(8,128)S(1)} %copy-done.1, ...), kind=kLoop, calls=%fused_computation.146 | loop fusion | flops 9934848 | bytes 41997824 | tf_op jit(solution)/shard_map/transpose(jvp())/mul | solution.py:16
  355.5 46.1 %pad_add_fusion = f32[1,34,34,704]{3,2,1,0:T(8,128)} fusion(f32[1,28,28,704]{3,2,1,0:T(8,128)} %get-tuple-element.154, f32[1,28,28,704]{3,2,1,0:T(8,128)} %get-tuple-element.155, f32[1,28,28,704]{3,2,1,0:T(8,128)} %get-tuple-element.156, f32[1,28,28,704]{3,2,1,0:T(8,128)} %get-tuple-element.157, f32[1,28,28,704]{3,2,1,0:T(8,128)} %get-tuple-element.158, ...), kind=kLoop, calls=%fused_computation.75 | loop fusion | flops 34180608 | bytes 98188288 | tf_op jit(solution)/shard_map/transpose(jvp())/add_any | solution.py:17
  401.6 8.9 %fusion.10 = bf16[1,28,28,704]{3,2,1,0:T(8,128)(2,1)} fusion(bf16[28,28,2816]{2,1,0:T(8,128)(2,1)} %reshape.863, bf16[2816,704]{1,0:T(8,128)(2,1)} %all-gather.5.cloned.1.call-done, bf16[1,28,28,704]{3,2,1,0:T(8,128)(2,1)S(1)} %copy-done.7), kind=kOutput, calls=%fused_computation.86 | convolution fusion | flops 3110159360 | bytes 10588160 | tf_op jit(solution)/shard_map/dot_general | solution.py:59
  410.5 38.9 %all-reduce.99 = (f32[704]{0:T(1024)S(1)}, f32[2816]{0:T(1024)S(1)}, f32[2816]{0:T(1024)S(1)}) all-reduce(f32[704]{0:T(1024)S(1)} %get-tuple-element.35, f32[2816]{0:T(1024)S(1)} %get-tuple-element.32, f32[2816]{0:T(1024)S(1)} %get-tuple-element.34), channel_id=1, replica_groups=mesh['rep'=8,'shard'=4] {'rep','shard'}, use_global_device_ids=true, to_apply=%region_59.60 | all-reduce | flops 6336 | bytes 50688 | tf_op jit(solution)/shard_map/psum | solution.py:85
  449.5 4.1 copy.23
  453.6 0.6 broadcast_multiply_fusion.53
  454.2 0.6 broadcast_multiply_fusion.51
  454.8 8.3 %fusion.9 = bf16[1,28,28,704]{3,2,1,0:T(8,128)(2,1)} fusion(f32[1,28,28,704]{3,2,1,0:T(8,128)S(1)} %copy-done.4, f32[1,28,28,704]{3,2,1,0:T(8,128)} %get-tuple-element.149, f32[1,28,28,704]{3,2,1,0:T(8,128)} %get-tuple-element.150, f32[1,28,28,704]{3,2,1,0:T(8,128)} %get-tuple-element.151, f32[1,28,28,704]{3,2,1,0:T(8,128)} %get-tuple-element.152, ...), kind=kLoop, calls=%fused_computation.79 | loop fusion | flops 4967424 | bytes 17661952 | tf_op jit(solution)/shard_map/convert_element_type | solution.py:75
  463.2 61.5 %all-reduce.103.cloned.1.call-done = f32[49,704]{1,0:T(8,128)} async-done(((f32[49,704]{1,0:T(8,128)}), f32[49,704]{1,0:T(8,128)}) %all-reduce.103.cloned.1.call-update) | async-done | bytes 138000 | tf_op jit(solution)/shard_map/psum | solution.py:85
  524.6 1.6 broadcast_multiply_fusion.49
  526.2 66.4 %all-reduce.105.cloned.1.call-done = bf16[704,1408]{0,1:T(8,128)(2,1)} async-done(((bf16[704,1408]{0,1:T(8,128)(2,1)}), bf16[704,1408]{0,1:T(8,128)(2,1)}) %all-reduce.105.cloned.1.call-update) | async-done | bytes 1982480 | tf_op jit(solution)/shard_map/psum | solution.py:84
  592.7 1.9 convert_element_type.51
  594.6 1.6 slice_multiply_fusion
  596.2 2.9 copy.21
  599.2 1.9 copy.20
  (233 shorter events, 2.3 us)
Async XLA Ops:
  7.2 7.3 %copy-start.5 = (bf16[1,28,28,704]{3,2,1,0:T(8,128)(2,1)S(1)}, bf16[1,28,28,704]{3,2,1,0:T(8,128)(2,1)}, u32[]{:S(2)}) copy-start(bf16[1,28,28,704]{3,2,1,0:T(8,128)(2,1)} %param.8) | copy-start | bytes 3311620
  7.2 88.0 %all-gather.3.cloned.1.call-start = ((), (), s32[]{:S(2)}) async-start(), calls=%async_computation.1 | async-start | bytes 5406720 | tf_op jit(solution)/shard_map/all_gather | solution.py:54
  7.9 170.3 %all-gather.5.cloned.1.call-start = ((), (), s32[]{:S(2)}) async-start(), calls=%async_computation.2 | async-start | bytes 5406720 | tf_op jit(solution)/shard_map/all_gather | solution.py:61
  8.7 440.8 %reduce-scatter.4.cloned.1.call-start = ((), (), s32[]{:S(2)}) async-start(), calls=%async_computation.5 | async-start | bytes 9912320
  9.8 6.6 %copy-start.10 = (f32[704]{0:T(1024)}, f32[704]{0:T(1024)S(1)}, u32[]{:S(2)}) copy-start(f32[704]{0:T(1024)S(1)} %get-tuple-element.124) | copy-start | bytes 8452
  91.6 86.6 %copy-start.82 = (f32[2816]{0:T(1024)S(1)}, f32[2816]{0:T(1024)}, u32[]{:S(2)}) copy-start(f32[2816]{0:T(1024)} %param.13) | copy-start | bytes 33796
  178.2 14.1 %copy-start.83 = (f32[2816]{0:T(1024)S(1)}, f32[2816]{0:T(1024)}, u32[]{:S(2)}) copy-start(f32[2816]{0:T(1024)} %param.14) | copy-start | bytes 33796
  258.6 266.0 %all-reduce.103.cloned.1.call-start = ((), (), s32[]{:S(2)}) async-start(), calls=%async_computation.3 | async-start | bytes 344064 | tf_op jit(solution)/shard_map/psum | solution.py:85
  283.9 12.1 %copy-start = (f32[1,28,28,704]{3,2,1,0:T(8,128)}, f32[1,28,28,704]{3,2,1,0:T(8,128)S(1)}, u32[]{:S(2)}) copy-start(f32[1,28,28,704]{3,2,1,0:T(8,128)S(1)} %get-tuple-element.138) | copy-start | bytes 6623236
  308.7 13.8 %copy-start.1 = (f32[1,28,28,704]{3,2,1,0:T(8,128)S(1)}, f32[1,28,28,704]{3,2,1,0:T(8,128)}, u32[]{:S(2)}) copy-start(f32[1,28,28,704]{3,2,1,0:T(8,128)} %copy-done) | copy-start | bytes 6623236
  308.7 13.8 %copy-start.47 = (f32[704]{0:T(1024)S(1)}, f32[704]{0:T(1024)}, u32[]{:S(2)}) copy-start(f32[704]{0:T(1024)} %copy-done.46) | copy-start | bytes 8452
  308.7 13.8 %copy-start.49 = (f32[704]{0:T(1024)S(1)}, f32[704]{0:T(1024)}, u32[]{:S(2)}) copy-start(f32[704]{0:T(1024)} %copy-done.48) | copy-start | bytes 8452
  308.7 13.8 %copy-start.51 = (f32[704]{0:T(1024)S(1)}, f32[704]{0:T(1024)}, u32[]{:S(2)}) copy-start(f32[704]{0:T(1024)} %copy-done.50) | copy-start | bytes 8452
  308.7 13.8 %copy-start.53 = (f32[704]{0:T(1024)S(1)}, f32[704]{0:T(1024)}, u32[]{:S(2)}) copy-start(f32[704]{0:T(1024)} %copy-done.52) | copy-start | bytes 8452
  308.8 13.8 %copy-start.55 = (f32[704]{0:T(1024)S(1)}, f32[704]{0:T(1024)}, u32[]{:S(2)}) copy-start(f32[704]{0:T(1024)} %copy-done.54) | copy-start | bytes 8452
  308.8 13.8 %copy-start.57 = (f32[704]{0:T(1024)S(1)}, f32[704]{0:T(1024)}, u32[]{:S(2)}) copy-start(f32[704]{0:T(1024)} %copy-done.56) | copy-start | bytes 8452
  308.8 13.8 %copy-start.59 = (f32[704]{0:T(1024)S(1)}, f32[704]{0:T(1024)}, u32[]{:S(2)}) copy-start(f32[704]{0:T(1024)} %copy-done.58) | copy-start | bytes 8452
  308.8 13.8 %copy-start.61 = (f32[704]{0:T(1024)S(1)}, f32[704]{0:T(1024)}, u32[]{:S(2)}) copy-start(f32[704]{0:T(1024)} %copy-done.60) | copy-start | bytes 8452
  308.8 13.8 %copy-start.63 = (f32[704]{0:T(1024)S(1)}, f32[704]{0:T(1024)}, u32[]{:S(2)}) copy-start(f32[704]{0:T(1024)} %copy-done.62) | copy-start | bytes 8452
  308.8 13.8 %copy-start.65 = (f32[704]{0:T(1024)S(1)}, f32[704]{0:T(1024)}, u32[]{:S(2)}) copy-start(f32[704]{0:T(1024)} %copy-done.64) | copy-start | bytes 8452
  308.8 13.8 %copy-start.67 = (f32[704]{0:T(1024)S(1)}, f32[704]{0:T(1024)}, u32[]{:S(2)}) copy-start(f32[704]{0:T(1024)} %copy-done.66) | copy-start | bytes 8452
  308.8 13.8 %copy-start.69 = (f32[704]{0:T(1024)S(1)}, f32[704]{0:T(1024)}, u32[]{:S(2)}) copy-start(f32[704]{0:T(1024)} %copy-done.68) | copy-start | bytes 8452
  308.8 13.8 %copy-start.71 = (f32[704]{0:T(1024)S(1)}, f32[704]{0:T(1024)}, u32[]{:S(2)}) copy-start(f32[704]{0:T(1024)} %copy-done.70) | copy-start | bytes 8452
  308.8 13.8 %copy-start.73 = (f32[704]{0:T(1024)S(1)}, f32[704]{0:T(1024)}, u32[]{:S(2)}) copy-start(f32[704]{0:T(1024)} %copy-done.72) | copy-start | bytes 8452
  308.9 13.8 %copy-start.75 = (f32[704]{0:T(1024)S(1)}, f32[704]{0:T(1024)}, u32[]{:S(2)}) copy-start(f32[704]{0:T(1024)} %copy-done.74) | copy-start | bytes 8452
  308.9 13.8 %copy-start.77 = (f32[704]{0:T(1024)S(1)}, f32[704]{0:T(1024)}, u32[]{:S(2)}) copy-start(f32[704]{0:T(1024)} %copy-done.76) | copy-start | bytes 8452
  308.9 13.8 %copy-start.79 = (f32[704]{0:T(1024)S(1)}, f32[704]{0:T(1024)}, u32[]{:S(2)}) copy-start(f32[704]{0:T(1024)} %copy-done.78) | copy-start | bytes 8452
  308.9 13.8 %copy-start.81 = (f32[704]{0:T(1024)S(1)}, f32[704]{0:T(1024)}, u32[]{:S(2)}) copy-start(f32[704]{0:T(1024)} %copy-done.80) | copy-start | bytes 8452
  322.7 16.3 %copy-start.11 = (f32[704]{0:T(1024)S(1)}, f32[704]{0:T(1024)}, u32[]{:S(2)}) copy-start(f32[704]{0:T(1024)} %copy-done.10) | copy-start | bytes 8452
  322.7 16.3 %copy-start.13 = (f32[704]{0:T(1024)S(1)}, f32[704]{0:T(1024)}, u32[]{:S(2)}) copy-start(f32[704]{0:T(1024)} %copy-done.12) | copy-start | bytes 8452
  322.7 16.3 %copy-start.15 = (f32[704]{0:T(1024)S(1)}, f32[704]{0:T(1024)}, u32[]{:S(2)}) copy-start(f32[704]{0:T(1024)} %copy-done.14) | copy-start | bytes 8452
  322.7 16.3 %copy-start.17 = (f32[704]{0:T(1024)S(1)}, f32[704]{0:T(1024)}, u32[]{:S(2)}) copy-start(f32[704]{0:T(1024)} %copy-done.16) | copy-start | bytes 8452
  322.7 16.3 %copy-start.19 = (f32[704]{0:T(1024)S(1)}, f32[704]{0:T(1024)}, u32[]{:S(2)}) copy-start(f32[704]{0:T(1024)} %copy-done.18) | copy-start | bytes 8452
  322.7 16.3 %copy-start.21 = (f32[704]{0:T(1024)S(1)}, f32[704]{0:T(1024)}, u32[]{:S(2)}) copy-start(f32[704]{0:T(1024)} %copy-done.20) | copy-start | bytes 8452
  322.7 16.3 %copy-start.23 = (f32[704]{0:T(1024)S(1)}, f32[704]{0:T(1024)}, u32[]{:S(2)}) copy-start(f32[704]{0:T(1024)} %copy-done.22) | copy-start | bytes 8452
  322.7 16.3 %copy-start.25 = (f32[704]{0:T(1024)S(1)}, f32[704]{0:T(1024)}, u32[]{:S(2)}) copy-start(f32[704]{0:T(1024)} %copy-done.24) | copy-start | bytes 8452
  322.8 16.3 %copy-start.27 = (f32[704]{0:T(1024)S(1)}, f32[704]{0:T(1024)}, u32[]{:S(2)}) copy-start(f32[704]{0:T(1024)} %copy-done.26) | copy-start | bytes 8452
  322.8 16.3 %copy-start.29 = (f32[704]{0:T(1024)S(1)}, f32[704]{0:T(1024)}, u32[]{:S(2)}) copy-start(f32[704]{0:T(1024)} %copy-done.28) | copy-start | bytes 8452
  322.8 16.3 %copy-start.31 = (f32[704]{0:T(1024)S(1)}, f32[704]{0:T(1024)}, u32[]{:S(2)}) copy-start(f32[704]{0:T(1024)} %copy-done.30) | copy-start | bytes 8452
  322.8 16.3 %copy-start.33 = (f32[704]{0:T(1024)S(1)}, f32[704]{0:T(1024)}, u32[]{:S(2)}) copy-start(f32[704]{0:T(1024)} %copy-done.32) | copy-start | bytes 8452
  322.8 16.3 %copy-start.35 = (f32[704]{0:T(1024)S(1)}, f32[704]{0:T(1024)}, u32[]{:S(2)}) copy-start(f32[704]{0:T(1024)} %copy-done.34) | copy-start | bytes 8452
  322.8 16.3 %copy-start.37 = (f32[704]{0:T(1024)S(1)}, f32[704]{0:T(1024)}, u32[]{:S(2)}) copy-start(f32[704]{0:T(1024)} %copy-done.36) | copy-start | bytes 8452
  322.8 16.3 %copy-start.39 = (f32[704]{0:T(1024)S(1)}, f32[704]{0:T(1024)}, u32[]{:S(2)}) copy-start(f32[704]{0:T(1024)} %copy-done.38) | copy-start | bytes 8452
  322.8 16.3 %copy-start.41 = (f32[704]{0:T(1024)S(1)}, f32[704]{0:T(1024)}, u32[]{:S(2)}) copy-start(f32[704]{0:T(1024)} %copy-done.40) | copy-start | bytes 8452
  322.8 16.3 %copy-start.43 = (f32[704]{0:T(1024)S(1)}, f32[704]{0:T(1024)}, u32[]{:S(2)}) copy-start(f32[704]{0:T(1024)} %copy-done.42) | copy-start | bytes 8452
  322.9 16.3 %copy-start.45 = (f32[704]{0:T(1024)S(1)}, f32[704]{0:T(1024)}, u32[]{:S(2)}) copy-start(f32[704]{0:T(1024)} %copy-done.44) | copy-start | bytes 8452
  355.4 237.2 %all-reduce.105.cloned.1.call-start = ((), (), s32[]{:S(2)}) async-start(), calls=%async_computation.4 | async-start | bytes 4325376 | tf_op jit(solution)/shard_map/psum | solution.py:84
  355.5 46.1 %copy-start.7 = (bf16[1,28,28,704]{3,2,1,0:T(8,128)(2,1)S(1)}, bf16[1,28,28,704]{3,2,1,0:T(8,128)(2,1)}, u32[]{:S(2)}) copy-start(bf16[1,28,28,704]{3,2,1,0:T(8,128)(2,1)} %param.8) | copy-start | bytes 3311620
  (41 other events, 182.5 us)
Sparse Core Ops, SparseCore 0:
  9.6 85.6 all-gather.2
  96.8 81.3 all-gather.4
  258.7 135.8 reduce-scatter.3
  400.6 124.0 all-reduce.102
  528.3 64.3 all-reduce.104
where the time goes:
time: 615 us; the launch traced here: 608 us
  other arithmetic  240 us (39%)
  waiting for transfers between devices  188 us (31%)
  matrix products  74.7 us (12%)
  local copies, waits for them, and re-layouts  48.2 us (8%)
  blocking collectives  38.9 us (6%)
  between operations  17 us (3%)
    reduce_sum x1, other arithmetic, stem_norm(): centre = jnp.mean(filtered, axis=-1, keepdims=True)  69.4 us
    psum x1, waiting for transfers between devices, shards(): summed = lax.psum(partial_sum, 'rep').astype(jnp.float32)  66.4 us
    psum x1, waiting for transfers between devices, shards(): lax.psum((back_kernel, back_gain, back_gamma, back_beta), ('rep', 'shard'))  61.5 us
    all_gather x1, waiting for transfers between devices, shards(): lax.all_gather(w_reduce, 'shard', axis=0, tiled=True)  55.5 us
    add_any x1, other arithmetic, stem_norm(): padded[:, offset_row:offset_row + height, offset_col:offset_col + breadth...  46.1 us
    mul x3, other arithmetic, stem_norm(): dw_kernel[offset_row * 7 + offset_col]  45.9 us
    dot_general x2, matrix products, against_rows(): lax.dot_general(left_cols, pieces, (((1,), (1,)), ((), ())), preferred_el...  39.1 us
    psum x1, blocking collectives, shards(): lax.psum((back_kernel, back_gain, back_gamma, back_beta), ('rep', 'shard'))  38.9 us
  transfers between devices with their start and end apart: 5, of which 4 were waited for; matrix products, arithmetic and copies ran while one was open for 45% of the time, Pallas kernels for 0%

commit v1 on v0

--- a/solution.py
+++ b/solution.py
@@ -82,7 +82,7 @@
         tiled=True,
     )
     summed = lax.psum(partial_sum, "rep").astype(jnp.float32)
-    reduced = lax.psum((back_kernel, back_gain, back_gamma, back_beta), ("rep", "shard"))
+    reduced = lax.psum(lax.psum((back_kernel, back_gain, back_gamma, back_beta), "shard"), "rep")
     inverse = 1.0 / (features.shape[0] * rep_count * shard_count)
     grad_expand = summed[:, :channels] * inverse
     grad_reduce = summed[:, channels:] * inverse

time: 615 us -> 587 us (0.954)
  waiting for transfers between devices: 188 us -> 157 us
    psum x1 -> x2, waiting for transfers between devices: 61.5 us -> 34.8 us  [the longest x1 34.7 us: shards(): lax.psum(lax.psum((back_kernel, back_gain, back_gamma, back_beta), 'shard...]
    unnamed x172 -> x180, local copies, waits for them, and re-layouts: 21.7 us -> 25.2 us
    psum x1 -> x2, blocking collectives: 38.9 us -> 41.6 us  [the longest x1 23.5 us: shards(): lax.psum(lax.psum((back_kernel, back_gain, back_gamma, back_beta), 'shard...]
  transfers between devices with their start and end apart: 5 -> 6, of which waited for: 4 -> 4; matrix products, arithmetic and copies ran while one was open for 45% -> 47% of each run, Pallas kernels for 0% -> 0%
where the time goes in v1:
time: 587 us; the launch traced here: 580 us
  other arithmetic  241 us (41%)
  waiting for transfers between devices  157 us (27%)
  matrix products  71 us (12%)
  local copies, waits for them, and re-layouts  51.2 us (9%)
  blocking collectives  41.6 us (7%)
  between operations  17.6 us (3%)
    reduce_sum x1, other arithmetic, stem_norm(): centre = jnp.mean(filtered, axis=-1, keepdims=True)  72.1 us
    psum x1, waiting for transfers between devices, shards(): summed = lax.psum(partial_sum, 'rep').astype(jnp.float32)  65.1 us
    all_gather x1, waiting for transfers between devices, shards(): lax.all_gather(w_reduce, 'shard', axis=0, tiled=True)  55 us
    add_any x1, other arithmetic, stem_norm(): padded[:, offset_row:offset_row + height, offset_col:offset_col + breadth...  46.7 us
    mul x3, other arithmetic, stem_norm(): dw_kernel[offset_row * 7 + offset_col]  44.6 us
    dot_general x2, matrix products, against_rows(): lax.dot_general(left_cols, pieces, (((1,), (1,)), ((), ())), preferred_el...  39.6 us
    psum x1, waiting for transfers between devices, shards(): lax.psum(lax.psum((back_kernel, back_gain, back_gamma, back_beta), 'shard...  34.7 us
    reduce_sum x3, other arithmetic, stem_norm(): dw_kernel[offset_row * 7 + offset_col]  31.2 us
  transfers between devices with their start and end apart: 6, of which 4 were waited for; matrix products, arithmetic and copies ran while one was open for 47% of the time, Pallas kernels for 0%

profile of v1, /device:TPU:0, one launch (start us, length us, event | category | flops | bytes accessed | tf_op | source)
XLA Modules:
  0.0 580.0 jit_solution(12946661223277956431)
XLA Ops:
  7.2 0.7 all-gather.3.cloned.1.call-update
  8.0 0.7 all-gather.5.cloned.1.call-update
  8.7 1.1 slice_reduce_fusion.46
  9.9 1.5 slice_reduce_fusion.48
  11.5 1.4 slice_reduce_fusion.47
  13.1 1.4 reshape.864
  14.5 1.9 convert_element_type.43
  16.7 72.1 %fusion.20 = (f32[28,28]{1,0:T(8,128)S(1)}, f32[1,28,28,704]{3,2,1,0:T(8,128)S(1)}) fusion(f32[704]{0:T(1024)S(1)} %get-tuple-element.133, f32[704]{0:T(1024)S(1)} %get-tuple-element.134, f32[704]{0:T(1024)S(1)} %get-tuple-element.87, f32[704]{0:T(1024)S(1)} %get-tuple-element.88, f32[704]{0:T(1024)S(1)} %get-tuple-element.89, ...), kind=kLoop, calls=%fused_computation.260 | loop fusion | flops 54088944 | bytes 4556608 | tf_op jit(solution)/shard_map/jvp()/reduce_sum | solution.py:19
  89.4 1.5 multiply_convert_fusion
  90.9 3.2 reshape.862
  94.1 1.1 all-gather.3.cloned.1.call-done
  95.2 26.6 %multiply_reduce_fusion.2 = (f32[2816]{0:T(1024)S(1)}, f32[784,2816]{1,0:T(8,128)}, f32[784,2816]{1,0:T(8,128)}) fusion(bf16[784,704]{1,0:T(8,128)(2,1)} %reshape.862, bf16[2816,704]{1,0:T(8,128)(2,1)} %all-gather.3.cloned.1.call-done), kind=kOutput, calls=%fused_computation.55 | convolution fusion | flops 3254211840 | bytes 22742016 | tf_op jit(solution)/shard_map/dot_general | solution.py:39
  123.1 55.0 %all-gather.5.cloned.1.call-done = bf16[2816,704]{1,0:T(8,128)(2,1)} async-done(((bf16[704,704]{1,0:T(8,128)(2,1)}), bf16[2816,704]{1,0:T(8,128)(2,1)}) %all-gather.5.cloned.1.call-update) | async-done | bytes 3964944 | tf_op jit(solution)/shard_map/all_gather | solution.py:61
  178.2 13.0 %multiply_reduce_fusion = (f32[2816]{0:T(1024)S(1)}, f32[2816]{0:T(1024)S(1)}, f32[2816]{0:T(1024)S(1)}, f32[784,2816]{1,0:T(8,128)}) fusion(f32[2816]{0:T(1024)S(1)} %fusion.17, f32[784,2816]{1,0:T(8,128)} %get-tuple-element.143, f32[784,2816]{1,0:T(8,128)} %get-tuple-element.199, f32[2816]{0:T(1024)S(1)} %copy-done.85, bf16[784,704]{1,0:T(8,128)(2,1)} %reshape.864, ...), kind=kOutput, calls=%fused_computation.51 | convolution fusion | flops 3128364800 | bytes 31618048 | tf_op jit(solution)/shard_map/dot_general | solution.py:39
  191.2 0.6 multiply_reduce_fusion.55
  192.5 14.6 %add_convert_fusion = (bf16[784,2816]{1,0:T(8,128)(2,1)S(1)}, bf16[784,2816]{1,0:T(8,128)(2,1)}) fusion(f32[784,2816]{1,0:T(8,128)} %get-tuple-element.143, f32[784,2816]{1,0:T(8,128)} %get-tuple-element.200, f32[784,2816]{1,0:T(8,128)} %get-tuple-element.199, f32[2816]{0:T(1024)S(1)} %multiply_multiply_fusion.7, f32[2816]{0:T(1024)S(1)} %fusion.17, ...), kind=kLoop, calls=%fused_computation.52 | loop fusion | flops 57401344 | bytes 35368960 | tf_op jit(solution)/shard_map/convert_element_type | solution.py:67
  207.0 2.1 copy-done.4
  209.1 5.0 fusion.21
  214.1 3.4 reshape.865
  217.6 2.6 multiply_reduce_fusion.53
  220.2 1.4 multiply_reduce_fusion.3
  222.3 8.0 %multiply_reduce_fusion.50 = (f32[704]{0:T(1024)S(1)}, f32[704]{0:T(1024)S(1)}, f32[704]{0:T(1024)S(1)}, f32[704]{0:T(1024)S(1)}, f32[704]{0:T(1024)S(1)}, /*ind...) fusion(f32[1,28,28,704]{3,2,1,0:T(8,128)S(1)} %copy-done.2, ...), kind=kLoop, calls=%fused_computation.134 | loop fusion | flops 18756672 | bytes 9986816 | tf_op jit(solution)/shard_map/transpose(jvp())/reduce_sum | solution.py:16
  230.3 11.3 %multiply_reduce_fusion.51 = (f32[704]{0:T(1024)S(1)}, f32[704]{0:T(1024)S(1)}, f32[704]{0:T(1024)S(1)}, f32[704]{0:T(1024)S(1)}, f32[704]{0:T(1024)S(1)}, /*ind...) fusion(f32[1,28,28,704]{3,2,1,0:T(8,128)S(1)} %get-tuple-elemen, ...), kind=kLoop, calls=%fused_computation.135 | loop fusion | flops 19857024 | bytes 4466176 | tf_op jit(solution)/shard_map/transpose(jvp())/reduce_sum | solution.py:16
  241.6 11.9 %multiply_reduce_fusion.52 = (f32[704]{0:T(1024)S(1)}, f32[704]{0:T(1024)S(1)}, f32[704]{0:T(1024)S(1)}, f32[704]{0:T(1024)S(1)}, f32[704]{0:T(1024)S(1)}, /*ind...) fusion(f32[1,28,28,704]{3,2,1,0:T(8,128)S(1)} %get-tuple-elemen, ...), kind=kLoop, calls=%fused_computation.136 | loop fusion | flops 19857024 | bytes 4466176 | tf_op jit(solution)/shard_map/transpose(jvp())/reduce_sum | solution.py:16
  253.5 6.8 %convert_element_type.50 = bf16[28,28,2816]{2,1,0:T(8,128)(2,1)} reshape(bf16[784,2816]{1,0:T(8,128)(2,1)} %copy-done.4) | data formatting | bytes 8830976 | tf_op jit(solution)/shard_map/convert_element_type | solution.py:67
  260.9 1.0 pad_add_fusion.7
  262.1 7.0 %reshape.863 = bf16[28,28,2816]{2,1,0:T(8,128)(2,1)} reshape(bf16[784,2816]{1,0:T(8,128)(2,1)} %get-tuple-element.147) | data formatting | bytes 8830976 | tf_op jit(solution)/shard_map/reshape.574
  269.0 8.8 %bitcast_convert_fusion = bf16[2816,704]{0,1:T(8,128)(2,1)} fusion(bf16[28,28,2816]{2,1,0:T(8,128)(2,1)} %reshape.863, bf16[1,28,28,704]{3,2,1,0:T(8,128)(2,1)S(1)} %copy-done.11), kind=kOutput, calls=%fused_computation.71 | convolution fusion | flops 3110486016 | bytes 9484288 | tf_op jit(solution)/shard_map/dot_general | solution.py:33
  277.9 8.6 %bitcast_convert_fusion.1 = bf16[2816,704]{0,1:T(8,128)(2,1)} fusion(bf16[28,28,2816]{2,1,0:T(8,128)(2,1)} %convert_element_type.50, bf16[1,28,28,704]{3,2,1,0:T(8,128)(2,1)S(1)} %copy-done.6), kind=kOutput, calls=%fused_computation.72 | convolution fusion | flops 3110486016 | bytes 9484288 | tf_op jit(solution)/shard_map/dot_general | solution.py:33
  286.5 7.0 %pad_maximum_fusion = bf16[2816,1408]{0,1:T(8,128)(2,1)} fusion(bf16[2816,704]{0,1:T(8,128)(2,1)} %bitcast_convert_fusion, bf16[2816,704]{0,1:T(8,128)(2,1)} %bitcast_convert_fusion.1), kind=kLoop, calls=%fused_computation.70 | loop fusion | flops 15859712 | bytes 15859712 | tf_op jit(solution)/shard_map/concatenate | solution.py:77
  293.6 11.3 %copy.22 = bf16[2816,1408]{1,0:T(8,128)(2,1)} copy(bf16[2816,1408]{0,1:T(8,128)(2,1)} %pad_maximum_fusion) | data formatting | bytes 15859712
  305.1 1.5 copy-done.1
  306.6 12.2 %broadcast_multiply_fusion.2 = (f32[1,28,28,704]{3,2,1,0:T(8,128)}, f32[1,28,28,704]{3,2,1,0:T(8,128)}, f32[1,28,28,704]{3,2,1,0:T(8,128)}, f32[1,28,28,704]{3,2...) fusion(f32[1,28,28,704]{3,2,1,0:T(8,128)S(1)} %copy-done.1, ...), kind=kLoop, calls=%fused_computation.148 | loop fusion | flops 7175168 | bytes 30945024 | tf_op jit(solution)/shard_map/transpose(jvp())/mul | solution.py:16
  319.2 16.1 %broadcast_multiply_fusion.1 = (f32[1,28,28,704]{3,2,1,0:T(8,128)}, f32[1,28,28,704]{3,2,1,0:T(8,128)}, f32[1,28,28,704]{3,2,1,0:T(8,128)}, f32[1,28,28,704]{3,2...) fusion(f32[1,28,28,704]{3,2,1,0:T(8,128)S(1)} %copy-done.1, ...), kind=kLoop, calls=%fused_computation.147 | loop fusion | flops 9934848 | bytes 41997824 | tf_op jit(solution)/shard_map/transpose(jvp())/mul | solution.py:16
  335.5 16.3 %broadcast_multiply_fusion = (f32[1,28,28,704]{3,2,1,0:T(8,128)}, f32[1,28,28,704]{3,2,1,0:T(8,128)}, f32[1,28,28,704]{3,2,1,0:T(8,128)}, f32[1,28,28,704]{3,2,1...) fusion(f32[1,28,28,704]{3,2,1,0:T(8,128)S(1)} %copy-done.1, ...), kind=kLoop, calls=%fused_computation.146 | loop fusion | flops 9934848 | bytes 41997824 | tf_op jit(solution)/shard_map/transpose(jvp())/mul | solution.py:16
  351.8 46.7 %pad_add_fusion = f32[1,34,34,704]{3,2,1,0:T(8,128)} fusion(f32[1,28,28,704]{3,2,1,0:T(8,128)} %get-tuple-element.157, f32[1,28,28,704]{3,2,1,0:T(8,128)} %get-tuple-element.158, f32[1,28,28,704]{3,2,1,0:T(8,128)} %get-tuple-element.159, f32[1,28,28,704]{3,2,1,0:T(8,128)} %get-tuple-element.160, f32[1,28,28,704]{3,2,1,0:T(8,128)} %get-tuple-element.161, ...), kind=kLoop, calls=%fused_computation.75 | loop fusion | flops 34180608 | bytes 98188288 | tf_op jit(solution)/shard_map/transpose(jvp())/add_any | solution.py:17
  398.6 9.0 %fusion.10 = bf16[1,28,28,704]{3,2,1,0:T(8,128)(2,1)} fusion(bf16[28,28,2816]{2,1,0:T(8,128)(2,1)} %reshape.863, bf16[2816,704]{1,0:T(8,128)(2,1)} %all-gather.5.cloned.1.call-done, bf16[1,28,28,704]{3,2,1,0:T(8,128)(2,1)S(1)} %copy-done.9), kind=kOutput, calls=%fused_computation.86 | convolution fusion | flops 3110159360 | bytes 10588160 | tf_op jit(solution)/shard_map/dot_general | solution.py:59
  407.6 18.1 %all-reduce.100 = (f32[704]{0:T(1024)S(1)}, f32[2816]{0:T(1024)S(1)}, f32[2816]{0:T(1024)S(1)}) all-reduce(f32[704]{0:T(1024)S(1)} %get-tuple-element.35, f32[2816]{0:T(1024)S(1)} %get-tuple-element.32, f32[2816]{0:T(1024)S(1)} %get-tuple-element.34), channel_id=1, replica_groups=mesh['rep'=8,'shard'=4] {'shard'}, use_global_device_ids=true, to_apply=%region_60.61 | all-reduce | flops 6336 | bytes 50688 | tf_op jit(solution)/shard_map/psum | solution.py:85
  425.7 23.5 %all-reduce.99 = (f32[704]{0:T(1024)S(1)}, f32[2816]{0:T(1024)S(1)}, f32[2816]{0:T(1024)S(1)}) all-reduce(f32[704]{0:T(1024)S(1)} %get-tuple-element.138, f32[2816]{0:T(1024)S(1)} %get-tuple-element.139, f32[2816]{0:T(1024)S(1)} %get-tuple-element.140), channel_id=1, replica_groups=mesh['rep'=8,'shard'=4] {'rep'}, use_global_device_ids=true, to_apply=%region_61.62 | all-reduce | flops 6336 | bytes 50688 | tf_op jit(solution)/shard_map/psum | solution.py:85
  449.2 4.1 copy.23
  454.5 8.3 %fusion.9 = bf16[1,28,28,704]{3,2,1,0:T(8,128)(2,1)} fusion(f32[1,28,28,704]{3,2,1,0:T(8,128)S(1)} %copy-done.5, f32[1,28,28,704]{3,2,1,0:T(8,128)} %get-tuple-element.152, f32[1,28,28,704]{3,2,1,0:T(8,128)} %get-tuple-element.153, f32[1,28,28,704]{3,2,1,0:T(8,128)} %get-tuple-element.154, f32[1,28,28,704]{3,2,1,0:T(8,128)} %get-tuple-element.155, ...), kind=kLoop, calls=%fused_computation.79 | loop fusion | flops 4967424 | bytes 17661952 | tf_op jit(solution)/shard_map/convert_element_type | solution.py:75
  462.9 34.7 %all-reduce.107.cloned.1.call-done = f32[49,704]{1,0:T(8,128)} async-done(((f32[49,704]{1,0:T(8,128)}), f32[49,704]{1,0:T(8,128)}) %all-reduce.107.cloned.1.call-update) | async-done | bytes 138000 | tf_op jit(solution)/shard_map/psum | solution.py:85
  497.6 1.6 broadcast_multiply_fusion.49
  499.2 65.1 %all-reduce.109.cloned.1.call-done = bf16[704,1408]{0,1:T(8,128)(2,1)} async-done(((bf16[704,1408]{0,1:T(8,128)(2,1)}), bf16[704,1408]{0,1:T(8,128)(2,1)}) %all-reduce.109.cloned.1.call-update) | async-done | bytes 1982480 | tf_op jit(solution)/shard_map/psum | solution.py:84
  564.3 1.9 convert_element_type.51
  566.3 1.6 slice_multiply_fusion
  567.9 2.9 copy.21
  570.8 1.9 copy.20
  (245 shorter events, 4.1 us)
Async XLA Ops:
  7.2 88.0 %all-gather.3.cloned.1.call-start = ((), (), s32[]{:S(2)}) async-start(), calls=%async_computation.1 | async-start | bytes 5406720 | tf_op jit(solution)/shard_map/all_gather | solution.py:54
  7.9 170.3 %all-gather.5.cloned.1.call-start = ((), (), s32[]{:S(2)}) async-start(), calls=%async_computation.2 | async-start | bytes 5406720 | tf_op jit(solution)/shard_map/all_gather | solution.py:61
  8.7 389.9 %all-reduce.105.cloned.1.call-start = ((), (), s32[]{:S(2)}) async-start(), calls=%async_computation.3 | async-start | bytes 344064 | tf_op jit(solution)/shard_map/psum | solution.py:85
  94.1 84.1 %copy-start.85 = (f32[2816]{0:T(1024)S(1)}, f32[2816]{0:T(1024)}, u32[]{:S(2)}) copy-start(f32[2816]{0:T(1024)} %param.13) | copy-start | bytes 33796
  178.2 14.2 %copy-start.86 = (f32[2816]{0:T(1024)S(1)}, f32[2816]{0:T(1024)}, u32[]{:S(2)}) copy-start(f32[2816]{0:T(1024)} %param.14) | copy-start | bytes 33796
  192.4 16.7 %copy-start.87 = (bf16[2816,704]{1,0:T(8,128)(2,1)S(1)}, bf16[2816,704]{1,0:T(8,128)(2,1)}, u32[]{:S(2)}) copy-start(bf16[2816,704]{1,0:T(8,128)(2,1)} %all-gather.3.cloned.1.call-done) | copy-start | bytes 11894788
  230.3 11.3 %copy-start = (f32[1,28,28,704]{3,2,1,0:T(8,128)}, f32[1,28,28,704]{3,2,1,0:T(8,128)S(1)}, u32[]{:S(2)}) copy-start(f32[1,28,28,704]{3,2,1,0:T(8,128)S(1)} %get-tuple-element.141) | copy-start | bytes 6623236
  262.0 187.2 %reduce-scatter.4.cloned.1.call-start = ((), (), s32[]{:S(2)}) async-start(), calls=%async_computation.6 | async-start | bytes 9912320
  269.0 8.8 %copy-start.6 = (bf16[1,28,28,704]{3,2,1,0:T(8,128)(2,1)S(1)}, bf16[1,28,28,704]{3,2,1,0:T(8,128)(2,1)}, u32[]{:S(2)}) copy-start(bf16[1,28,28,704]{3,2,1,0:T(8,128)(2,1)} %multiply_convert_fusion) | copy-start | bytes 3311620
  304.8 14.0 %copy-start.50 = (f32[704]{0:T(1024)S(1)}, f32[704]{0:T(1024)}, u32[]{:S(2)}) copy-start(f32[704]{0:T(1024)} %copy-done.49) | copy-start | bytes 8452
  304.9 14.0 %copy-start.52 = (f32[704]{0:T(1024)S(1)}, f32[704]{0:T(1024)}, u32[]{:S(2)}) copy-start(f32[704]{0:T(1024)} %copy-done.51) | copy-start | bytes 8452
  304.9 14.0 %copy-start.54 = (f32[704]{0:T(1024)S(1)}, f32[704]{0:T(1024)}, u32[]{:S(2)}) copy-start(f32[704]{0:T(1024)} %copy-done.53) | copy-start | bytes 8452
  304.9 14.0 %copy-start.56 = (f32[704]{0:T(1024)S(1)}, f32[704]{0:T(1024)}, u32[]{:S(2)}) copy-start(f32[704]{0:T(1024)} %copy-done.55) | copy-start | bytes 8452
  304.9 14.0 %copy-start.58 = (f32[704]{0:T(1024)S(1)}, f32[704]{0:T(1024)}, u32[]{:S(2)}) copy-start(f32[704]{0:T(1024)} %copy-done.57) | copy-start | bytes 8452
  304.9 14.0 %copy-start.60 = (f32[704]{0:T(1024)S(1)}, f32[704]{0:T(1024)}, u32[]{:S(2)}) copy-start(f32[704]{0:T(1024)} %copy-done.59) | copy-start | bytes 8452
  304.9 14.0 %copy-start.62 = (f32[704]{0:T(1024)S(1)}, f32[704]{0:T(1024)}, u32[]{:S(2)}) copy-start(f32[704]{0:T(1024)} %copy-done.61) | copy-start | bytes 8452
  304.9 14.0 %copy-start.64 = (f32[704]{0:T(1024)S(1)}, f32[704]{0:T(1024)}, u32[]{:S(2)}) copy-start(f32[704]{0:T(1024)} %copy-done.63) | copy-start | bytes 8452
  304.9 14.0 %copy-start.66 = (f32[704]{0:T(1024)S(1)}, f32[704]{0:T(1024)}, u32[]{:S(2)}) copy-start(f32[704]{0:T(1024)} %copy-done.65) | copy-start | bytes 8452
  304.9 14.0 %copy-start.68 = (f32[704]{0:T(1024)S(1)}, f32[704]{0:T(1024)}, u32[]{:S(2)}) copy-start(f32[704]{0:T(1024)} %copy-done.67) | copy-start | bytes 8452
  304.9 14.0 %copy-start.70 = (f32[704]{0:T(1024)S(1)}, f32[704]{0:T(1024)}, u32[]{:S(2)}) copy-start(f32[704]{0:T(1024)} %copy-done.69) | copy-start | bytes 8452
  305.0 14.0 %copy-start.72 = (f32[704]{0:T(1024)S(1)}, f32[704]{0:T(1024)}, u32[]{:S(2)}) copy-start(f32[704]{0:T(1024)} %copy-done.71) | copy-start | bytes 8452
  305.0 14.0 %copy-start.74 = (f32[704]{0:T(1024)S(1)}, f32[704]{0:T(1024)}, u32[]{:S(2)}) copy-start(f32[704]{0:T(1024)} %copy-done.73) | copy-start | bytes 8452
  305.0 14.0 %copy-start.76 = (f32[704]{0:T(1024)S(1)}, f32[704]{0:T(1024)}, u32[]{:S(2)}) copy-start(f32[704]{0:T(1024)} %copy-done.75) | copy-start | bytes 8452
  305.0 14.0 %copy-start.78 = (f32[704]{0:T(1024)S(1)}, f32[704]{0:T(1024)}, u32[]{:S(2)}) copy-start(f32[704]{0:T(1024)} %copy-done.77) | copy-start | bytes 8452
  305.0 14.0 %copy-start.80 = (f32[704]{0:T(1024)S(1)}, f32[704]{0:T(1024)}, u32[]{:S(2)}) copy-start(f32[704]{0:T(1024)} %copy-done.79) | copy-start | bytes 8452
  305.0 14.0 %copy-start.82 = (f32[704]{0:T(1024)S(1)}, f32[704]{0:T(1024)}, u32[]{:S(2)}) copy-start(f32[704]{0:T(1024)} %copy-done.81) | copy-start | bytes 8452
  305.0 14.0 %copy-start.84 = (f32[704]{0:T(1024)S(1)}, f32[704]{0:T(1024)}, u32[]{:S(2)}) copy-start(f32[704]{0:T(1024)} %copy-done.83) | copy-start | bytes 8452
  305.0 192.6 %all-reduce.107.cloned.1.call-start = ((), (), s32[]{:S(2)}) async-start(), calls=%async_computation.4 | async-start | bytes 344064 | tf_op jit(solution)/shard_map/psum | solution.py:85
  319.0 16.3 %copy-start.14 = (f32[704]{0:T(1024)S(1)}, f32[704]{0:T(1024)}, u32[]{:S(2)}) copy-start(f32[704]{0:T(1024)} %copy-done.13) | copy-start | bytes 8452
  319.0 16.3 %copy-start.16 = (f32[704]{0:T(1024)S(1)}, f32[704]{0:T(1024)}, u32[]{:S(2)}) copy-start(f32[704]{0:T(1024)} %copy-done.15) | copy-start | bytes 8452
  319.0 16.3 %copy-start.18 = (f32[704]{0:T(1024)S(1)}, f32[704]{0:T(1024)}, u32[]{:S(2)}) copy-start(f32[704]{0:T(1024)} %copy-done.17) | copy-start | bytes 8452
  319.0 16.3 %copy-start.20 = (f32[704]{0:T(1024)S(1)}, f32[704]{0:T(1024)}, u32[]{:S(2)}) copy-start(f32[704]{0:T(1024)} %copy-done.19) | copy-start | bytes 8452
  319.1 16.3 %copy-start.22 = (f32[704]{0:T(1024)S(1)}, f32[704]{0:T(1024)}, u32[]{:S(2)}) copy-start(f32[704]{0:T(1024)} %copy-done.21) | copy-start | bytes 8452
  319.1 16.3 %copy-start.24 = (f32[704]{0:T(1024)S(1)}, f32[704]{0:T(1024)}, u32[]{:S(2)}) copy-start(f32[704]{0:T(1024)} %copy-done.23) | copy-start | bytes 8452
  319.1 16.3 %copy-start.26 = (f32[704]{0:T(1024)S(1)}, f32[704]{0:T(1024)}, u32[]{:S(2)}) copy-start(f32[704]{0:T(1024)} %copy-done.25) | copy-start | bytes 8452
  319.1 16.3 %copy-start.28 = (f32[704]{0:T(1024)S(1)}, f32[704]{0:T(1024)}, u32[]{:S(2)}) copy-start(f32[704]{0:T(1024)} %copy-done.27) | copy-start | bytes 8452
  319.1 16.3 %copy-start.30 = (f32[704]{0:T(1024)S(1)}, f32[704]{0:T(1024)}, u32[]{:S(2)}) copy-start(f32[704]{0:T(1024)} %copy-done.29) | copy-start | bytes 8452
  319.1 16.3 %copy-start.32 = (f32[704]{0:T(1024)S(1)}, f32[704]{0:T(1024)}, u32[]{:S(2)}) copy-start(f32[704]{0:T(1024)} %copy-done.31) | copy-start | bytes 8452
  319.1 16.3 %copy-start.34 = (f32[704]{0:T(1024)S(1)}, f32[704]{0:T(1024)}, u32[]{:S(2)}) copy-start(f32[704]{0:T(1024)} %copy-done.33) | copy-start | bytes 8452
  319.1 16.3 %copy-start.36 = (f32[704]{0:T(1024)S(1)}, f32[704]{0:T(1024)}, u32[]{:S(2)}) copy-start(f32[704]{0:T(1024)} %copy-done.35) | copy-start | bytes 8452
  319.1 16.3 %copy-start.38 = (f32[704]{0:T(1024)S(1)}, f32[704]{0:T(1024)}, u32[]{:S(2)}) copy-start(f32[704]{0:T(1024)} %copy-done.37) | copy-start | bytes 8452
  319.1 16.3 %copy-start.40 = (f32[704]{0:T(1024)S(1)}, f32[704]{0:T(1024)}, u32[]{:S(2)}) copy-start(f32[704]{0:T(1024)} %copy-done.39) | copy-start | bytes 8452
  319.2 16.3 %copy-start.42 = (f32[704]{0:T(1024)S(1)}, f32[704]{0:T(1024)}, u32[]{:S(2)}) copy-start(f32[704]{0:T(1024)} %copy-done.41) | copy-start | bytes 8452
  319.2 16.3 %copy-start.44 = (f32[704]{0:T(1024)S(1)}, f32[704]{0:T(1024)}, u32[]{:S(2)}) copy-start(f32[704]{0:T(1024)} %copy-done.43) | copy-start | bytes 8452
  319.2 16.3 %copy-start.46 = (f32[704]{0:T(1024)S(1)}, f32[704]{0:T(1024)}, u32[]{:S(2)}) copy-start(f32[704]{0:T(1024)} %copy-done.45) | copy-start | bytes 8452
  319.2 16.3 %copy-start.48 = (f32[704]{0:T(1024)S(1)}, f32[704]{0:T(1024)}, u32[]{:S(2)}) copy-start(f32[704]{0:T(1024)} %copy-done.47) | copy-start | bytes 8452
  351.8 46.8 %copy-start.9 = (bf16[1,28,28,704]{3,2,1,0:T(8,128)(2,1)S(1)}, bf16[1,28,28,704]{3,2,1,0:T(8,128)(2,1)}, u32[]{:S(2)}) copy-start(bf16[1,28,28,704]{3,2,1,0:T(8,128)(2,1)} %param.8) | copy-start | bytes 3311620
  398.6 165.7 %all-reduce.109.cloned.1.call-start = ((), (), s32[]{:S(2)}) async-start(), calls=%async_computation.5 | async-start | bytes 4325376 | tf_op jit(solution)/shard_map/psum | solution.py:84
  (46 other events, 205.1 us)
Sparse Core Ops, SparseCore 0:
  9.6 85.6 all-gather.2
  96.8 81.3 all-gather.4
  262.1 33.0 all-reduce.104
  305.0 136.8 reduce-scatter.3
  444.8 52.7 all-reduce.106
  501.3 62.9 all-reduce.108
